TPU v7x, 128 devices: a whole 4x4x4 slice. The times are simulated.
128 devices in a mesh: row: 16 (over y, z), col: 8 (over x, core).
Axes of the slice: x: 4, y: 4, z: 4, core: 2. Of those that a mesh axis runs over, the one named last changes fastest.
Arguments:
- descriptors: bfloat16 [131072, 512], P(('row', 'col')), may hold values from -6 to 6
- center_index: int32 [16384], replicated, may hold values from 0 to 131071, as said below
- panel_index: int32 [1], replicated, may hold values from 0 to 15
Outputs:
- schur: float32 [16384, 16384], P('row', 'col')
- panel_factor: float32 [16384, 1024], P('row', 'col')
Inputs may be any that keep to these rules, and one draw needn't show every extreme that they name: Center j is row center_index[j] mod 1024 of shard center_index[j] // 1024, shards numbered row-major over row and col. In each aligned run of 128 centers no shard supplies more than 4 centers, and some shard supplies exactly 4.
All inputs are finite; a program needn't handle non-finite values.
Results may differ from a plain program's by a relative error of at most 0.0003.
Values may be sent and summed in bfloat16 or wider, within the bound.
No kernel may reach another device: no remote copies, remote signals or barrier semaphores. Data moves between devices by JAX's collectives and lax.ppermute only.
A program may use at most 128 MiB of HBM per device.

v0:
```python
import jax
import jax.numpy as jnp
from jax import lax
from jax.sharding import PartitionSpec as P

D = 512
PANEL = 1024
GROUP = 128
ridge = 1.0


def broadcast(block, axis, holder):
    block = jnp.where(lax.axis_index(axis) == holder, block, jnp.zeros_like(block))
    return lax.psum(block, axis)


def gram_block(left, right, left_sq, right_sq):
    inner = lax.dot_general(
        left, right, (((1,), (1,)), ((), ())), preferred_element_type=jnp.float32
    )
    return jnp.exp(-(left_sq[:, None] + right_sq[None, :] - 2.0 * inner) / D)


def squares(values):
    return jnp.sum(jnp.square(values.astype(jnp.float32)), axis=1)


def transposed_product(left, right):
    return lax.dot_general(
        left,
        right,
        (((1,), (1,)), ((), ())),
        precision=lax.Precision.HIGHEST,
        preferred_element_type=jnp.float32,
    )


def body(descriptors, center_index, panel_index):
    rows_axis = lax.axis_size("row")
    cols_axis = lax.axis_size("col")
    device_count = rows_axis * cols_axis
    my_row = lax.axis_index("row")
    my_col = lax.axis_index("col")
    my_flat = my_row * cols_axis + my_col
    data_rows = descriptors.shape[0]
    capacity = max(4, 2 * GROUP // device_count)
    tile_rows = GROUP * cols_axis
    by_group = center_index.reshape(device_count, GROUP)
    shard_of = by_group // data_rows
    same_shard = shard_of[:, :, None] == shard_of[:, None, :]
    earlier = (
        jnp.arange(GROUP, dtype=jnp.int32)[None, :] < jnp.arange(GROUP, dtype=jnp.int32)[:, None]
    )
    slot_rank = jnp.sum((same_shard & earlier[None, :, :]).astype(jnp.int32), axis=2)
    targets = jnp.where(
        shard_of == my_flat,
        jnp.arange(device_count, dtype=jnp.int32)[:, None] * capacity + slot_rank,
        device_count * capacity,
    )
    local_row = by_group - my_flat * data_rows
    slot_rows = (
        jnp.zeros((device_count * capacity,), jnp.int32)
        .at[targets.reshape(-1)]
        .set(local_row.reshape(-1), mode="drop")
    )
    outgoing = jnp.take(descriptors, slot_rows, axis=0)
    arrived = lax.all_to_all(
        outgoing.reshape(device_count, capacity, D),
        ("row", "col"),
        split_axis=0,
        concat_axis=0,
        tiled=True,
    )
    my_shards = lax.dynamic_index_in_dim(shard_of, my_flat, 0, keepdims=False)
    my_ranks = lax.dynamic_index_in_dim(slot_rank, my_flat, 0, keepdims=False)
    my_centers = arrived[my_shards, my_ranks]
    row_centers = lax.all_gather(my_centers, "col", axis=0, tiled=True)
    col_centers = lax.all_gather(my_centers, "row", axis=0, tiled=True)
    row_sq = squares(row_centers)
    col_sq = squares(col_centers)
    row_pos = my_row * tile_rows + jnp.arange(tile_rows, dtype=jnp.int32)
    col_pos = (
        (jnp.arange(rows_axis, dtype=jnp.int32)[:, None] * cols_axis + my_col) * GROUP
        + jnp.arange(GROUP, dtype=jnp.int32)[None, :]
    ).reshape(-1)
    tile = gram_block(row_centers, col_centers, row_sq, col_sq)
    tile = tile + ridge * (row_pos[:, None] == col_pos[None, :]).astype(jnp.float32)
    start_pos = panel_index[0] * PANEL
    first_pos = start_pos + 0
    owner_row = first_pos // tile_rows
    pieces = broadcast(row_centers, "row", owner_row)
    panel_sq = squares(pieces)
    panel_pos = start_pos + jnp.arange(PANEL, dtype=jnp.int32)
    diag_block = gram_block(pieces, pieces, panel_sq, panel_sq) + ridge * jnp.eye(
        PANEL, dtype=jnp.float32
    )
    diag_factor = jnp.linalg.cholesky(diag_block)
    row_block = gram_block(row_centers, pieces, row_sq, panel_sq)
    row_block = row_block + ridge * (row_pos[:, None] == panel_pos[None, :]).astype(jnp.float32)
    row_factor = lax.linalg.triangular_solve(
        diag_factor, row_block, left_side=False, lower=True, transpose_a=True
    )
    own_rows = lax.dynamic_slice_in_dim(row_factor, my_col * GROUP, GROUP, 0)
    schur = tile - transposed_product(
        row_factor, lax.all_gather(own_rows, "row", axis=0, tiled=True)
    )
    share = PANEL // cols_axis
    panel_factor = lax.dynamic_slice_in_dim(row_factor, my_col * share, share, 1)
    return (schur, panel_factor)


def solution(mesh):
    return jax.shard_map(
        body,
        mesh=mesh,
        in_specs=(P(("row", "col"), None), P(), P()),
        out_specs=(P("row", "col"), P("row", "col")),
        check_vma=False,
    )
```

profile of v0, /device:TPU:0, one launch (start us, length us, event | category | flops | bytes accessed | tf_op | source)
XLA Modules:
  0.0 700.6 jit_solution(14249034032198965943)
XLA Ops:
  14.3 60.3 %scatter_custom_fusion = s32[512]{0:T(512)S(1)} fusion(s32[16384]{0:T(1024)S(1)} %get-tuple-element.74, s32[16384]{0:T(1024)S(1)} %get-tuple-element.73, s32[]{:T(128)} %copy.83), kind=kCustom, calls=%fused_computation.197 | custom fusion | bytes 2052 | tf_op jit(solution)/shard_map/scatter | solution.py:64
  78.0 11.2 %all-to-all-start = ((bf16[128,4,512]{2,1,0:T(4,128)(2,1)}), bf16[128,4,512]{2,1,0:T(4,128)(2,1)S(1)}, u32[]{:S(2)}, u32[]{:S(2)}) async-start(bf16[128,4,512]{2,1,0:T(4,128)(2,1)} %broadcast_select_fusion.1), calls=%async_computation | async-start | bytes 1048576 | tf_op jit(solution)/shard_map/all_to_all | solution.py:67
  89.2 13.4 %all-to-all-done = bf16[128,4,512]{2,1,0:T(4,128)(2,1)S(1)} async-done(((bf16[128,4,512]{2,1,0:T(4,128)(2,1)}), bf16[128,4,512]{2,1,0:T(4,128)(2,1)S(1)}, u32[]{:S(2)}, u32[]{:S(2)}) %all-to-all-start) | async-done | bytes 524320 | tf_op jit(solution)/shard_map/all_to_all | solution.py:67
  105.4 18.7 %all-gather.4.cloned.1.call-done = bf16[1024,512]{1,0:T(8,128)(2,1)} async-done(((bf16[128,512]{1,0:T(8,128)(2,1)}), bf16[1024,512]{1,0:T(8,128)(2,1)}) %all-gather.4.cloned.1.call-update) | async-done | bytes 1048592 | tf_op jit(solution)/shard_map/all_gather | solution.py:77
  127.4 87.8 %all-reduce.3.cloned.1.call-done = bf16[1024,512]{1,0:T(8,128)(2,1)} async-done(((bf16[1024,512]{1,0:T(8,128)(2,1)}), bf16[1024,512]{1,0:T(8,128)(2,1)}) %all-reduce.3.cloned.1.call-update) | async-done | bytes 1048592 | tf_op jit(solution)/shard_map/psum | solution.py:14
  243.1 11.7 %cholesky.223 = f32[128,128]{1,0:T(8,128)S(1)} custom-call(f32[128,128]{1,0:T(8,128)S(1)} %cholesky.580), custom_call_target="Cholesky" | custom-call | tf_op jit(solution)/shard_map/jit(cholesky)/cholesky | solution.py:97
  257.4 9.8 %custom-call.62 = f32[1,128,128]{1,2,0:T(8,128)S(1)} custom-call(f32[1,128,128]{2,1,0:T(8,128)S(1)} %get-tuple-element.72), custom_call_target="InvertDiagBlocksLowerTriangular" | custom-call | tf_op jit(solution)/shard_map/jit(cholesky)/cholesky | solution.py:97
  271.1 11.7 %cholesky.244 = f32[128,128]{1,0:T(8,128)S(1)} custom-call(f32[128,128]{1,0:T(8,128)S(1)} %cholesky.584), custom_call_target="Cholesky" | custom-call | tf_op jit(solution)/shard_map/jit(cholesky)/cholesky | solution.py:97
  283.4 10.0 %custom-call.63 = f32[1,128,128]{1,2,0:T(8,128)S(1)} custom-call(f32[1,128,128]{2,1,0:T(8,128)S(1)} %get-tuple-element.69), custom_call_target="InvertDiagBlocksLowerTriangular" | custom-call | tf_op jit(solution)/shard_map/jit(cholesky)/cholesky | solution.py:97
  296.7 11.7 %cholesky.468 = f32[128,128]{1,0:T(8,128)S(1)} custom-call(f32[128,128]{1,0:T(8,128)S(1)} %cholesky.589), custom_call_target="Cholesky" | custom-call | tf_op jit(solution)/shard_map/jit(cholesky)/cholesky | solution.py:97
  309.7 9.8 %custom-call.64 = f32[1,128,128]{1,2,0:T(8,128)S(1)} custom-call(f32[1,128,128]{2,1,0:T(8,128)S(1)} %get-tuple-element.66), custom_call_target="InvertDiagBlocksLowerTriangular" | custom-call | tf_op jit(solution)/shard_map/jit(cholesky)/cholesky | solution.py:97
  323.1 12.1 %cholesky.487 = f32[128,128]{1,0:T(8,128)S(1)} custom-call(f32[128,128]{1,0:T(8,128)S(1)} %cholesky.594), custom_call_target="Cholesky" | custom-call | tf_op jit(solution)/shard_map/jit(cholesky)/cholesky | solution.py:97
  336.5 9.8 %custom-call.65 = f32[1,128,128]{1,2,0:T(8,128)S(1)} custom-call(f32[1,128,128]{2,1,0:T(8,128)S(1)} %get-tuple-element.63), custom_call_target="InvertDiagBlocksLowerTriangular" | custom-call | tf_op jit(solution)/shard_map/jit(cholesky)/cholesky | solution.py:97
  349.7 11.7 %cholesky.506 = f32[128,128]{1,0:T(8,128)S(1)} custom-call(f32[128,128]{1,0:T(8,128)S(1)} %cholesky.599), custom_call_target="Cholesky" | custom-call | tf_op jit(solution)/shard_map/jit(cholesky)/cholesky | solution.py:97
  362.8 9.8 %custom-call.66 = f32[1,128,128]{1,2,0:T(8,128)S(1)} custom-call(f32[1,128,128]{2,1,0:T(8,128)S(1)} %get-tuple-element.60), custom_call_target="InvertDiagBlocksLowerTriangular" | custom-call | tf_op jit(solution)/shard_map/jit(cholesky)/cholesky | solution.py:97
  376.1 11.7 %cholesky.526 = f32[128,128]{1,0:T(8,128)S(1)} custom-call(f32[128,128]{1,0:T(8,128)S(1)} %cholesky.604), custom_call_target="Cholesky" | custom-call | tf_op jit(solution)/shard_map/jit(cholesky)/cholesky | solution.py:97
  389.0 9.8 %custom-call.67 = f32[1,128,128]{1,2,0:T(8,128)S(1)} custom-call(f32[1,128,128]{2,1,0:T(8,128)S(1)} %get-tuple-element.57), custom_call_target="InvertDiagBlocksLowerTriangular" | custom-call | tf_op jit(solution)/shard_map/jit(cholesky)/cholesky | solution.py:97
  401.9 11.7 %cholesky.546 = f32[128,128]{1,0:T(8,128)S(1)} custom-call(f32[128,128]{1,0:T(8,128)S(1)} %cholesky.609), custom_call_target="Cholesky" | custom-call | tf_op jit(solution)/shard_map/jit(cholesky)/cholesky | solution.py:97
  414.9 10.0 %custom-call.68 = f32[1,128,128]{1,2,0:T(8,128)S(1)} custom-call(f32[1,128,128]{2,1,0:T(8,128)S(1)} %get-tuple-element.54), custom_call_target="InvertDiagBlocksLowerTriangular" | custom-call | tf_op jit(solution)/shard_map/jit(cholesky)/cholesky | solution.py:97
  427.6 11.7 %cholesky.564 = f32[128,128]{1,0:T(8,128)S(1)} custom-call(f32[128,128]{1,0:T(8,128)S(1)} %convolution_subtract_fusion.11), custom_call_target="Cholesky" | custom-call | tf_op jit(solution)/shard_map/jit(cholesky)/cholesky | solution.py:97
  451.3 24.1 %while.1 = (s32[]{:T(128)}, f32[1024,1024]{1,0:T(8,128)}, s32[8,2]{0,1:T(2,128)S(1)}, f32[8,128,128]{2,1,0:T(8,128)S(1)}, s32[]{:T(128)}) while((s32[]{:T(128)}, f32[1024,1024]{1,0:T(8,128)}, s32[8,2]{0,1:T(2,128)S(1)}, f32[8,128,128]{2,1,0:T(8,128)S(1)}, s32[]{:T(128)}) %tuple.67), condition=%wide.while_cond, body=%wide.while_body.sunk | while | flops 2 | bytes 131181 | solution.py:100
  475.4 79.0 %custom-call.69 = f32[8,128,128]{1,2,0:T(8,128)S(1)} custom-call(f32[8,128,128]{2,1,0:T(8,128)S(1)} %get-tuple-element.9), custom_call_target="InvertDiagBlocksLowerTriangular" | custom-call | tf_op jit(solution)/shard_map/triangular_solve | solution.py:100
  585.4 72.5 %all-gather.8.cloned.1.call-done = f32[2048,1024]{0,1:T(8,128)} async-done(((f32[128,1024]{0,1:T(8,128)}), f32[2048,1024]{0,1:T(8,128)}) %all-gather.8.cloned.1.call-update) | async-done | bytes 8388624 | tf_op jit(solution)/shard_map/all_gather | solution.py:105
  657.9 29.8 %fusion.80 = f32[1024,2048]{1,0:T(8,128)S(1)} fusion(f32[1024,1024]{0,1:T(8,128)} %copy-done.6, f32[2048,1024]{0,1:T(8,128)} %all-gather.8.cloned.1.call-done), kind=kOutput, calls=%fused_computation.212 | convolution fusion | flops 25769803776 | bytes 20971520 | tf_op jit(solution)/shard_map/dot_general | solution.py:29
  (134 shorter events, 144.5 us)
Async XLA Ops:
  7.2 67.4 %copy-start = (bf16[1024,512]{1,0:T(8,128)(2,1)S(1)}, bf16[1024,512]{1,0:T(8,128)(2,1)}, u32[]{:S(2)}) copy-start(bf16[1024,512]{1,0:T(8,128)(2,1)} %param.3) | copy-start | bytes 3145732
  78.0 24.7 %all-to-all-start = ((bf16[128,4,512]{2,1,0:T(4,128)(2,1)}), bf16[128,4,512]{2,1,0:T(4,128)(2,1)S(1)}, u32[]{:S(2)}, u32[]{:S(2)}) async-start(bf16[128,4,512]{2,1,0:T(4,128)(2,1)} %broadcast_select_fusion.1), calls=%async_computation | async-start | bytes 1048576 | tf_op jit(solution)/shard_map/all_to_all | solution.py:67
  89.2 34.9 %all-gather.4.cloned.1.call-start = ((), (), s32[]{:S(2)}) async-start(), calls=%async_computation.1 | async-start | bytes 1179648 | tf_op jit(solution)/shard_map/all_gather | solution.py:77
  104.6 110.6 %all-reduce.3.cloned.1.call-start = ((), (), s32[]{:S(2)}) async-start(), calls=%async_computation.3 | async-start | bytes 2097152 | tf_op jit(solution)/shard_map/psum | solution.py:14
  125.1 458.3 %all-gather.6.cloned.1.call-start = ((), (), s32[]{:S(2)}) async-start(), calls=%async_computation.2 | async-start | bytes 2228224 | tf_op jit(solution)/shard_map/all_gather | solution.py:78
  125.8 532.1 %all-gather.8.cloned.1.call-start = ((), (), s32[]{:S(2)}) async-start(), calls=%async_computation.4 | async-start | bytes 8912896 | tf_op jit(solution)/shard_map/all_gather | solution.py:105
  241.2 1.9 copy-start.2
  446.2 108.2 %copy-start.3 = (bf16[1024,512]{1,0:T(8,128)(2,1)S(1)}, bf16[1024,512]{1,0:T(8,128)(2,1)}, u32[]{:S(2)}) copy-start(bf16[1024,512]{1,0:T(8,128)(2,1)} %all-reduce.3.cloned.1.call-done) | copy-start | bytes 3145732
  446.2 108.2 %copy-start.4 = (bf16[1024,512]{1,0:T(8,128)(2,1)S(1)}, bf16[1024,512]{1,0:T(8,128)(2,1)}, u32[]{:S(2)}) copy-start(bf16[1024,512]{1,0:T(8,128)(2,1)} %all-gather.4.cloned.1.call-done) | copy-start | bytes 3145732
  578.2 2.0 copy-start.6
  657.9 29.8 %copy-start.5 = (bf16[2048,512]{1,0:T(8,128)(2,1)S(1)}, bf16[2048,512]{1,0:T(8,128)(2,1)}, u32[]{:S(2)}) copy-start(bf16[2048,512]{1,0:T(8,128)(2,1)} %all-gather.6.cloned.1.call-done) | copy-start | bytes 6291460
  687.8 6.1 copy-start.1
Sparse Core Ops, SparseCore 0:
  104.8 19.2 all-gather.3
  127.9 87.3 all-reduce.2
  217.4 44.5 all-gather.5
  581.3 76.5 all-gather.7
where the time goes:
time: 708 us; the launch traced here: 701 us
  other arithmetic  277 us (39%)
  waiting for transfers between devices  193 us (27%)
  local copies, waits for them, and re-layouts  109 us (15%)
  matrix products  90.4 us (13%)
  between operations  20.1 us (3%)
  starting transfers between devices  11.3 us (2%)
    another operation x30, other arithmetic, body(): diag_factor = jnp.linalg.cholesky(diag_block)  172 us
    psum x1, waiting for transfers between devices, broadcast(): return lax.psum(block, axis)  87.8 us
    another operation x3, other arithmetic, body(): lax.linalg.triangular_solve(diag_factor, row_block, left_side=False, lowe...  84 us
    all_gather x1, waiting for transfers between devices, body(): lax.all_gather(own_rows, 'row', axis=0, tiled=True)  72.5 us
    scatter x1, local copies, waits for them, and re-layouts, body(): slot_rows = jnp.zeros((device_count * capacity,), jnp.int32).at[targets.r...  60.3 us
    dot_general x1, matrix products, transposed_product(): lax.dot_general(left, right, (((1,), (1,)), ((), ())), precision=lax.Prec...  29.8 us
    another operation x24, local copies, waits for them, and re-layouts  24 us
    another operation x14, matrix products, body(): diag_factor = jnp.linalg.cholesky(diag_block)  23.2 us
  transfers between devices with their start and end apart: 5, of which 4 were waited for; matrix products, arithmetic and copies ran while one was open for 52% of the time, Pallas kernels for 0%

commit v1 on v0

--- a/solution.py
+++ b/solution.py
@@ -7,6 +7,28 @@
 PANEL = 1024
 GROUP = 128
 ridge = 1.0
+
+
+def joined_along(blocks, dim):
+    lengths = list(blocks.shape[1:])
+    lengths[dim] *= blocks.shape[0]
+    return jnp.moveaxis(blocks, 0, dim).reshape(lengths)
+
+
+def gather_around(x, axis, dim):
+    devices = lax.axis_size(axis)
+    pairs = [(i, (i + 1) % devices) for i in range(devices)]
+    back = [(b, a) for a, b in pairs]
+    lower, upper = ([], [])
+    for step in range(devices - 1):
+        if step % 2 == 0:
+            lower.append(lax.ppermute(lower[-1] if lower else x, axis, pairs))
+        else:
+            upper.append(lax.ppermute(upper[-1] if upper else x, axis, back))
+    blocks = jnp.stack([*lower[::-1], x, *upper])
+    shift = lax.axis_index(axis) - len(lower)
+    blocks = blocks[(jnp.arange(devices) - shift) % devices]
+    return joined_along(blocks, dim)
 
 
 def broadcast(block, axis, holder):
@@ -101,9 +123,7 @@
         diag_factor, row_block, left_side=False, lower=True, transpose_a=True
     )
     own_rows = lax.dynamic_slice_in_dim(row_factor, my_col * GROUP, GROUP, 0)
-    schur = tile - transposed_product(
-        row_factor, lax.all_gather(own_rows, "row", axis=0, tiled=True)
-    )
+    schur = tile - transposed_product(row_factor, gather_around(own_rows, "row", 0))
     share = PANEL // cols_axis
     panel_factor = lax.dynamic_slice_in_dim(row_factor, my_col * share, share, 1)
     return (schur, panel_factor)

time: 708 us -> 817 us (1.15)
  starting transfers between devices: 11.3 us -> 50.4 us
  local copies, waits for them, and re-layouts: 109 us -> 145 us
  matrix products: 90.4 us -> 117 us
    ppermute x0 -> x15, waiting for transfers between devices: none -> 76.3 us  [the longest x8 74 us: gather_around(): lower.append(lax.ppermute(lower[-1] if lower else x, axis, pairs))]
    all_gather x1 -> x0, waiting for transfers between devices: 72.5 us -> none  [body(): lax.all_gather(own_rows, 'row', axis=0, tiled=True)]
    ppermute x0 -> x15, starting transfers between devices: none -> 39.2 us  [the longest x7 38 us: gather_around(): upper.append(lax.ppermute(upper[-1] if upper else x, axis, back))]
    dot_general x1, matrix products: 29.8 us -> 55.8 us  [transposed_product(): lax.dot_general(left, right, (((1,), (1,)), ((), ())), precision=lax.Prec...]
    unnamed x15 -> x50, local copies, waits for them, and re-layouts: 4.95 us -> 24.7 us
    gather x0 -> x2, local copies, waits for them, and re-layouts: none -> 16.9 us  [gather_around(): blocks = blocks[(jnp.arange(devices) - shift) % devices]]
    another operation x24 -> x25, local copies, waits for them, and re-layouts: 24 us -> 24.8 us
  transfers between devices with their start and end apart: 5 -> 19, of which waited for: 4 -> 12; matrix products, arithmetic and copies ran while one was open for 52% -> 3% of each run, Pallas kernels for 0% -> 0%
where the time goes in v1:
time: 817 us; the launch traced here: 807 us
  other arithmetic  277 us (34%)
  waiting for transfers between devices  197 us (24%)
  local copies, waits for them, and re-layouts  145 us (18%)
  matrix products  117 us (14%)
  starting transfers between devices  50.4 us (6%)
  between operations  20.2 us (2%)
    another operation x30, other arithmetic, body(): diag_factor = jnp.linalg.cholesky(diag_block)  172 us
    psum x1, waiting for transfers between devices, broadcast(): return lax.psum(block, axis)  88.5 us
    another operation x3, other arithmetic, body(): lax.linalg.triangular_solve(diag_factor, row_block, left_side=False, lowe...  83.8 us
    ppermute x8, waiting for transfers between devices, gather_around(): lower.append(lax.ppermute(lower[-1] if lower else x, axis, pairs))  74 us
    scatter x1, local copies, waits for them, and re-layouts, body(): slot_rows = jnp.zeros((device_count * capacity,), jnp.int32).at[targets.r...  60.3 us
    dot_general x1, matrix products, transposed_product(): lax.dot_general(left, right, (((1,), (1,)), ((), ())), precision=lax.Prec...  55.8 us
    ppermute x7, starting transfers between devices, gather_around(): upper.append(lax.ppermute(upper[-1] if upper else x, axis, back))  38 us
    unnamed x50, local copies, waits for them, and re-layouts  24.7 us
  transfers between devices with their start and end apart: 19, of which 12 were waited for; matrix products, arithmetic and copies ran while one was open for 3% of the time, Pallas kernels for 0%

profile of v1, /device:TPU:0, one launch (start us, length us, event | category | flops | bytes accessed | tf_op | source)
XLA Modules:
  0.0 806.6 jit_solution(7102787759243249244)
XLA Ops:
  14.3 60.3 %scatter_custom_fusion = s32[512]{0:T(512)S(1)} fusion(s32[16384]{0:T(1024)S(1)} %get-tuple-element.74, s32[16384]{0:T(1024)S(1)} %get-tuple-element.73, s32[]{:T(128)} %copy.100), kind=kCustom, calls=%fused_computation.219 | custom fusion | bytes 2052 | tf_op jit(solution)/shard_map/scatter | solution.py:86
  78.0 11.2 %all-to-all-start = ((bf16[128,4,512]{2,1,0:T(4,128)(2,1)}), bf16[128,4,512]{2,1,0:T(4,128)(2,1)S(1)}, u32[]{:S(2)}, u32[]{:S(2)}) async-start(bf16[128,4,512]{2,1,0:T(4,128)(2,1)} %broadcast_select_fusion.1), calls=%async_computation | async-start | bytes 1048576 | tf_op jit(solution)/shard_map/all_to_all | solution.py:89
  89.2 13.4 %all-to-all-done = bf16[128,4,512]{2,1,0:T(4,128)(2,1)S(1)} async-done(((bf16[128,4,512]{2,1,0:T(4,128)(2,1)}), bf16[128,4,512]{2,1,0:T(4,128)(2,1)S(1)}, u32[]{:S(2)}, u32[]{:S(2)}) %all-to-all-start) | async-done | bytes 524320 | tf_op jit(solution)/shard_map/all_to_all | solution.py:89
  105.4 18.7 %all-gather.3.cloned.1.call-done = bf16[1024,512]{1,0:T(8,128)(2,1)} async-done(((bf16[128,512]{1,0:T(8,128)(2,1)}), bf16[1024,512]{1,0:T(8,128)(2,1)}) %all-gather.3.cloned.1.call-update) | async-done | bytes 1048592 | tf_op jit(solution)/shard_map/all_gather | solution.py:99
  126.7 88.5 %all-reduce.3.cloned.1.call-done = bf16[1024,512]{1,0:T(8,128)(2,1)} async-done(((bf16[1024,512]{1,0:T(8,128)(2,1)}), bf16[1024,512]{1,0:T(8,128)(2,1)}) %all-reduce.3.cloned.1.call-update) | async-done | bytes 1048592 | tf_op jit(solution)/shard_map/psum | solution.py:36
  243.3 11.7 %cholesky.223 = f32[128,128]{1,0:T(8,128)S(1)} custom-call(f32[128,128]{1,0:T(8,128)S(1)} %cholesky.580), custom_call_target="Cholesky" | custom-call | tf_op jit(solution)/shard_map/jit(cholesky)/cholesky | solution.py:119
  271.2 11.7 %cholesky.244 = f32[128,128]{1,0:T(8,128)S(1)} custom-call(f32[128,128]{1,0:T(8,128)S(1)} %cholesky.584), custom_call_target="Cholesky" | custom-call | tf_op jit(solution)/shard_map/jit(cholesky)/cholesky | solution.py:119
  283.6 9.9 %custom-call.63 = f32[1,128,128]{1,2,0:T(8,128)S(1)} custom-call(f32[1,128,128]{2,1,0:T(8,128)S(1)} %get-tuple-element.69), custom_call_target="InvertDiagBlocksLowerTriangular" | custom-call | tf_op jit(solution)/shard_map/jit(cholesky)/cholesky | solution.py:119
  296.9 11.7 %cholesky.468 = f32[128,128]{1,0:T(8,128)S(1)} custom-call(f32[128,128]{1,0:T(8,128)S(1)} %cholesky.589), custom_call_target="Cholesky" | custom-call | tf_op jit(solution)/shard_map/jit(cholesky)/cholesky | solution.py:119
  323.2 11.9 %cholesky.487 = f32[128,128]{1,0:T(8,128)S(1)} custom-call(f32[128,128]{1,0:T(8,128)S(1)} %cholesky.594), custom_call_target="Cholesky" | custom-call | tf_op jit(solution)/shard_map/jit(cholesky)/cholesky | solution.py:119
  336.4 9.8 %custom-call.65 = f32[1,128,128]{1,2,0:T(8,128)S(1)} custom-call(f32[1,128,128]{2,1,0:T(8,128)S(1)} %get-tuple-element.63), custom_call_target="InvertDiagBlocksLowerTriangular" | custom-call | tf_op jit(solution)/shard_map/jit(cholesky)/cholesky | solution.py:119
  349.6 11.7 %cholesky.506 = f32[128,128]{1,0:T(8,128)S(1)} custom-call(f32[128,128]{1,0:T(8,128)S(1)} %cholesky.599), custom_call_target="Cholesky" | custom-call | tf_op jit(solution)/shard_map/jit(cholesky)/cholesky | solution.py:119
  362.7 9.8 %custom-call.66 = f32[1,128,128]{1,2,0:T(8,128)S(1)} custom-call(f32[1,128,128]{2,1,0:T(8,128)S(1)} %get-tuple-element.60), custom_call_target="InvertDiagBlocksLowerTriangular" | custom-call | tf_op jit(solution)/shard_map/jit(cholesky)/cholesky | solution.py:119
  376.2 11.7 %cholesky.526 = f32[128,128]{1,0:T(8,128)S(1)} custom-call(f32[128,128]{1,0:T(8,128)S(1)} %cholesky.604), custom_call_target="Cholesky" | custom-call | tf_op jit(solution)/shard_map/jit(cholesky)/cholesky | solution.py:119
  402.1 11.7 %cholesky.546 = f32[128,128]{1,0:T(8,128)S(1)} custom-call(f32[128,128]{1,0:T(8,128)S(1)} %cholesky.609), custom_call_target="Cholesky" | custom-call | tf_op jit(solution)/shard_map/jit(cholesky)/cholesky | solution.py:119
  415.1 10.0 %custom-call.68 = f32[1,128,128]{1,2,0:T(8,128)S(1)} custom-call(f32[1,128,128]{2,1,0:T(8,128)S(1)} %get-tuple-element.54), custom_call_target="InvertDiagBlocksLowerTriangular" | custom-call | tf_op jit(solution)/shard_map/jit(cholesky)/cholesky | solution.py:119
  427.7 11.7 %cholesky.564 = f32[128,128]{1,0:T(8,128)S(1)} custom-call(f32[128,128]{1,0:T(8,128)S(1)} %convolution_subtract_fusion.11), custom_call_target="Cholesky" | custom-call | tf_op jit(solution)/shard_map/jit(cholesky)/cholesky | solution.py:119
  451.4 24.1 %while.1 = (s32[]{:T(128)}, f32[1024,1024]{1,0:T(8,128)}, s32[8,2]{0,1:T(2,128)S(1)}, f32[8,128,128]{2,1,0:T(8,128)S(1)}, s32[]{:T(128)}) while((s32[]{:T(128)}, f32[1024,1024]{1,0:T(8,128)}, s32[8,2]{0,1:T(2,128)S(1)}, f32[8,128,128]{2,1,0:T(8,128)S(1)}, s32[]{:T(128)}) %tuple.67), condition=%wide.while_cond, body=%wide.while_body.sunk | while | flops 2 | bytes 131181 | solution.py:122
  475.5 78.8 %custom-call.69 = f32[8,128,128]{1,2,0:T(8,128)S(1)} custom-call(f32[8,128,128]{2,1,0:T(8,128)S(1)} %get-tuple-element.9), custom_call_target="InvertDiagBlocksLowerTriangular" | custom-call | tf_op jit(solution)/shard_map/triangular_solve | solution.py:122
  581.7 14.5 %collective-permute-done = f32[128,1024]{0,1:T(8,128)S(1)} collective-permute-done((f32[128,1024]{0,1:T(8,128)S(1)}, f32[128,1024]{0,1:T(8,128)S(1)}, u32[]{:S(2)}, u32[]{:S(2)}) %collective-permute-start) | collective-permute-done | bytes 524320 | tf_op jit(solution)/shard_map/ppermute | solution.py:25
  601.5 10.8 %collective-permute-done.1 = f32[128,1024]{0,1:T(8,128)S(1)} collective-permute-done((f32[128,1024]{0,1:T(8,128)S(1)}, f32[128,1024]{0,1:T(8,128)S(1)}, u32[]{:S(2)}, u32[]{:S(2)}) %collective-permute-start.1) | collective-permute-done | bytes 524320 | tf_op jit(solution)/shard_map/ppermute | solution.py:25
  617.7 10.7 %collective-permute-done.2 = f32[128,1024]{0,1:T(8,128)S(1)} collective-permute-done((f32[128,1024]{0,1:T(8,128)S(1)}, f32[128,1024]{0,1:T(8,128)S(1)}, u32[]{:S(2)}, u32[]{:S(2)}) %collective-permute-start.2) | collective-permute-done | bytes 524320 | tf_op jit(solution)/shard_map/ppermute | solution.py:25
  636.4 10.3 %collective-permute-done.3 = f32[128,1024]{0,1:T(8,128)S(1)} collective-permute-done((f32[128,1024]{0,1:T(8,128)S(1)}, f32[128,1024]{0,1:T(8,128)S(1)}, u32[]{:S(2)}, u32[]{:S(2)}) %collective-permute-start.3) | collective-permute-done | bytes 524320 | tf_op jit(solution)/shard_map/ppermute | solution.py:25
  738.0 55.8 %fusion.82 = f32[1024,2048]{1,0:T(8,128)S(1)} fusion(f32[1024,1024]{0,1:T(8,128)} %copy-done.6, f32[2048,1024]{1,0:T(8,128)} %bitcast.181), kind=kOutput, calls=%fused_computation.236 | convolution fusion | flops 25769803776 | bytes 20971520 | tf_op jit(solution)/shard_map/dot_general | solution.py:51
  (201 shorter events, 279.9 us)
Async XLA Ops:
  7.2 67.4 %copy-start = (bf16[1024,512]{1,0:T(8,128)(2,1)S(1)}, bf16[1024,512]{1,0:T(8,128)(2,1)}, u32[]{:S(2)}) copy-start(bf16[1024,512]{1,0:T(8,128)(2,1)} %param.3) | copy-start | bytes 3145732
  78.0 24.7 %all-to-all-start = ((bf16[128,4,512]{2,1,0:T(4,128)(2,1)}), bf16[128,4,512]{2,1,0:T(4,128)(2,1)S(1)}, u32[]{:S(2)}, u32[]{:S(2)}) async-start(bf16[128,4,512]{2,1,0:T(4,128)(2,1)} %broadcast_select_fusion.1), calls=%async_computation | async-start | bytes 1048576 | tf_op jit(solution)/shard_map/all_to_all | solution.py:89
  89.2 34.9 %all-gather.3.cloned.1.call-start = ((), (), s32[]{:S(2)}) async-start(), calls=%async_computation.1 | async-start | bytes 1179648 | tf_op jit(solution)/shard_map/all_gather | solution.py:99
  104.6 110.6 %all-reduce.3.cloned.1.call-start = ((), (), s32[]{:S(2)}) async-start(), calls=%async_computation.3 | async-start | bytes 2097152 | tf_op jit(solution)/shard_map/psum | solution.py:36
  125.1 564.7 %all-gather.5.cloned.1.call-start = ((), (), s32[]{:S(2)}) async-start(), calls=%async_computation.2 | async-start | bytes 2228224 | tf_op jit(solution)/shard_map/all_gather | solution.py:100
  446.3 108.0 %copy-start.3 = (bf16[1024,512]{1,0:T(8,128)(2,1)S(1)}, bf16[1024,512]{1,0:T(8,128)(2,1)}, u32[]{:S(2)}) copy-start(bf16[1024,512]{1,0:T(8,128)(2,1)} %all-reduce.3.cloned.1.call-done) | copy-start | bytes 3145732
  446.3 108.0 %copy-start.4 = (bf16[1024,512]{1,0:T(8,128)(2,1)S(1)}, bf16[1024,512]{1,0:T(8,128)(2,1)}, u32[]{:S(2)}) copy-start(bf16[1024,512]{1,0:T(8,128)(2,1)} %all-gather.3.cloned.1.call-done) | copy-start | bytes 3145732
  580.5 15.7 %collective-permute-start = (f32[128,1024]{0,1:T(8,128)S(1)}, f32[128,1024]{0,1:T(8,128)S(1)}, u32[]{:S(2)}, u32[]{:S(2)}) collective-permute-start(f32[128,1024]{0,1:T(8,128)S(1)} %constant_dynamic-slice_fusion.2), channel_id=1, source_target_pairs={{0,8},{8,16},{16,24},{24,32},{32,40},{40,48},{48,56},{56,64},{64,7... | collective-permute-start | bytes 1572872 | tf_op jit(solution)/shard_map/ppermute | solution.py:25
  596.2 16.2 %collective-permute-start.1 = (f32[128,1024]{0,1:T(8,128)S(1)}, f32[128,1024]{0,1:T(8,128)S(1)}, u32[]{:S(2)}, u32[]{:S(2)}) collective-permute-start(f32[128,1024]{0,1:T(8,128)S(1)} %collective-permute-done), channel_id=1, source_target_pairs={{0,8},{8,16},{16,24},{24,32},{32,40},{40,48},{48,56},{56,64},{64,7... | collective-permute-start | bytes 1572872 | tf_op jit(solution)/shard_map/ppermute | solution.py:25
  596.2 16.2 %collective-permute-start.8 = (f32[128,1024]{0,1:T(8,128)S(1)}, f32[128,1024]{0,1:T(8,128)S(1)}, u32[]{:S(2)}, u32[]{:S(2)}) collective-permute-start(f32[128,1024]{0,1:T(8,128)S(1)} %constant_dynamic-slice_fusion.2), channel_id=1, source_target_pairs={{8,0},{16,8},{24,16},{32,24},{40,32},{48,40},{56,48},{64,56},{72,6... | collective-permute-start | bytes 1572872 | tf_op jit(solution)/shard_map/ppermute | solution.py:27
  612.4 16.0 %collective-permute-start.2 = (f32[128,1024]{0,1:T(8,128)S(1)}, f32[128,1024]{0,1:T(8,128)S(1)}, u32[]{:S(2)}, u32[]{:S(2)}) collective-permute-start(f32[128,1024]{0,1:T(8,128)S(1)} %collective-permute-done.1), channel_id=1, source_target_pairs={{0,8},{8,16},{16,24},{24,32},{32,40},{40,48},{48,56},{56,64},{64,7... | collective-permute-start | bytes 1572872 | tf_op jit(solution)/shard_map/ppermute | solution.py:25
  612.4 18.2 %collective-permute-start.9 = (f32[128,1024]{0,1:T(8,128)S(1)}, f32[128,1024]{0,1:T(8,128)S(1)}, u32[]{:S(2)}, u32[]{:S(2)}) collective-permute-start(f32[128,1024]{0,1:T(8,128)S(1)} %collective-permute-done.8), channel_id=1, source_target_pairs={{8,0},{16,8},{24,16},{32,24},{40,32},{48,40},{56,48},{64,56},{72,6... | collective-permute-start | bytes 1572872 | tf_op jit(solution)/shard_map/ppermute | solution.py:27
  628.4 18.4 %collective-permute-start.3 = (f32[128,1024]{0,1:T(8,128)S(1)}, f32[128,1024]{0,1:T(8,128)S(1)}, u32[]{:S(2)}, u32[]{:S(2)}) collective-permute-start(f32[128,1024]{0,1:T(8,128)S(1)} %collective-permute-done.2), channel_id=1, source_target_pairs={{0,8},{8,16},{16,24},{24,32},{32,40},{40,48},{48,56},{56,64},{64,7... | collective-permute-start | bytes 1572872 | tf_op jit(solution)/shard_map/ppermute | solution.py:25
  630.6 57.0 %copy-start.7 = (f32[128,1024]{0,1:T(8,128)}, f32[128,1024]{0,1:T(8,128)S(1)}, u32[]{:S(2)}) copy-start(f32[128,1024]{0,1:T(8,128)S(1)} %collective-permute-done.9) | copy-start | bytes 1572868
  630.6 16.1 %collective-permute-start.10 = (f32[128,1024]{0,1:T(8,128)S(1)}, f32[128,1024]{0,1:T(8,128)S(1)}, u32[]{:S(2)}, u32[]{:S(2)}) collective-permute-start(f32[128,1024]{0,1:T(8,128)S(1)} %collective-permute-done.9), channel_id=1, source_target_pairs={{8,0},{16,8},{24,16},{32,24},{40,32},{48,40},{56,48},{64,56},{72,6... | collective-permute-start | bytes 1572872 | tf_op jit(solution)/shard_map/ppermute | solution.py:27
  646.7 14.3 %collective-permute-start.4 = (f32[128,1024]{0,1:T(8,128)S(1)}, f32[128,1024]{0,1:T(8,128)S(1)}, u32[]{:S(2)}, u32[]{:S(2)}) collective-permute-start(f32[128,1024]{0,1:T(8,128)S(1)} %collective-permute-done.3), channel_id=1, source_target_pairs={{0,8},{8,16},{16,24},{24,32},{32,40},{40,48},{48,56},{56,64},{64,7... | collective-permute-start | bytes 1572872 | tf_op jit(solution)/shard_map/ppermute | solution.py:25
  646.8 14.3 %collective-permute-start.11 = (f32[128,1024]{0,1:T(8,128)S(1)}, f32[128,1024]{0,1:T(8,128)}, u32[]{:S(2)}, u32[]{:S(2)}) collective-permute-start(f32[128,1024]{0,1:T(8,128)S(1)} %collective-permute-done.10), channel_id=1, source_target_pairs={{8,0},{16,8},{24,16},{32,24},{40,32},{48,40},{56,48},{64,56},{72,6... | collective-permute-start | bytes 1572872 | tf_op jit(solution)/shard_map/ppermute | solution.py:27
  661.1 13.6 %collective-permute-start.5 = (f32[128,1024]{0,1:T(8,128)S(1)}, f32[128,1024]{0,1:T(8,128)}, u32[]{:S(2)}, u32[]{:S(2)}) collective-permute-start(f32[128,1024]{0,1:T(8,128)S(1)} %collective-permute-done.4), channel_id=1, source_target_pairs={{0,8},{8,16},{16,24},{24,32},{32,40},{40,48},{48,56},{56,64},{64,7... | collective-permute-start | bytes 1572872 | tf_op jit(solution)/shard_map/ppermute | solution.py:25
  661.1 13.7 %collective-permute-start.12 = (f32[128,1024]{0,1:T(8,128)}, f32[128,1024]{0,1:T(8,128)}, u32[]{:S(2)}, u32[]{:S(2)}) collective-permute-start(f32[128,1024]{0,1:T(8,128)} %collective-permute-done.11), channel_id=1, source_target_pairs={{8,0},{16,8},{24,16},{32,24},{40,32},{48,40},{56,48},{64,56},{72,6... | collective-permute-start | bytes 1572872 | tf_op jit(solution)/shard_map/ppermute | solution.py:27
  674.7 12.9 %collective-permute-start.6 = (f32[128,1024]{0,1:T(8,128)}, f32[128,1024]{0,1:T(8,128)}, u32[]{:S(2)}, u32[]{:S(2)}) collective-permute-start(f32[128,1024]{0,1:T(8,128)} %collective-permute-done.5), channel_id=1, source_target_pairs={{0,8},{8,16},{16,24},{24,32},{32,40},{40,48},{48,56},{56,64},{64,7... | collective-permute-start | bytes 1572872 | tf_op jit(solution)/shard_map/ppermute | solution.py:25
  674.8 17.2 %collective-permute-start.13 = (f32[128,1024]{0,1:T(8,128)}, f32[128,1024]{0,1:T(8,128)}, u32[]{:S(2)}, u32[]{:S(2)}) collective-permute-start(f32[128,1024]{0,1:T(8,128)} %collective-permute-done.12), channel_id=1, source_target_pairs={{8,0},{16,8},{24,16},{32,24},{40,32},{48,40},{56,48},{64,56},{72,6... | collective-permute-start | bytes 1572872 | tf_op jit(solution)/shard_map/ppermute | solution.py:27
  687.6 12.8 %collective-permute-start.7 = (f32[128,1024]{0,1:T(8,128)}, f32[128,1024]{0,1:T(8,128)}, u32[]{:S(2)}, u32[]{:S(2)}) collective-permute-start(f32[128,1024]{0,1:T(8,128)} %collective-permute-done.6), channel_id=1, source_target_pairs={{0,8},{8,16},{16,24},{24,32},{32,40},{40,48},{48,56},{56,64},{64,7... | collective-permute-start | bytes 1572872 | tf_op jit(solution)/shard_map/ppermute | solution.py:25
  692.0 28.2 %collective-permute-start.14 = (f32[128,1024]{0,1:T(8,128)}, f32[128,1024]{0,1:T(8,128)S(1)}, u32[]{:S(2)}, u32[]{:S(2)}) collective-permute-start(f32[128,1024]{0,1:T(8,128)} %collective-permute-done.13), channel_id=1, source_target_pairs={{8,0},{16,8},{24,16},{32,24},{40,32},{48,40},{56,48},{64,56},{72,6... | collective-permute-start | bytes 1572872 | tf_op jit(solution)/shard_map/ppermute | solution.py:27
  738.0 55.8 %copy-start.5 = (bf16[2048,512]{1,0:T(8,128)(2,1)S(1)}, bf16[2048,512]{1,0:T(8,128)(2,1)}, u32[]{:S(2)}) copy-start(bf16[2048,512]{1,0:T(8,128)(2,1)} %all-gather.5.cloned.1.call-done) | copy-start | bytes 6291460
  (12 other events, 121.5 us)
Sparse Core Ops, SparseCore 0:
  104.8 19.2 all-gather.2
  127.9 87.3 all-reduce.2
  581.8 61.4 all-gather.4
